TPU v7x, 128 devices: a whole 4x4x4 slice. The times are simulated.
128 devices in a mesh: row: 16 (over x, z), col: 8 (over y, core).
Axes of the slice: x: 4, y: 4, z: 4, core: 2. Of those that a mesh axis runs over, the one named last changes fastest.
Arguments:
- qkv: bfloat16 [3, 1408, 32768], P(None, 'col', 'row'), may hold values from -12.1 to 12.1
- residual_in: bfloat16 [1408, 32768], P('col', 'row'), may hold values from -3 to 3
- out_weight: bfloat16 [1408, 1408], replicated, may hold values from -0.625 to 0.625
- merge_weight: bfloat16 [1408, 5632], P('col'), may hold values from -0.078125 to 0.078125
- merge_gain: float32 [1408], replicated, may hold values from 0.1 to 1.9
- image_groups: int32 [64], replicated, may hold values from 1 to 256, 8192 in all
- dest_row: int32 [8192], P('row'), may hold values from 0 to 8191, as said below
Outputs:
- layer_out: bfloat16 [1408, 32768], P('col', 'row')
- image_rows: bfloat16 [1408, 8192], P('col', 'row')
Inputs may be any that keep to these rules, and one draw needn't show every extreme that they name: dest_row is a permutation of 0 to 8191. Of the 512 entries held by each index of row, exactly 32 fall in each aligned block of 512 output rows.
All inputs are finite; a program needn't handle non-finite values.
Results may differ from a plain program's by a relative error of at most 0.0064.
Values may be sent and summed in bfloat16 or wider, within the bound.
A program may use at most 128 MiB of HBM per device.

v0:
```python
import math
import jax
import jax.numpy as jnp
from jax import lax
from jax.sharding import PartitionSpec as P

HEAD_DIM = 88


def with_halo(cells, sides, width):
    for axis, dim in sides:
        count = lax.axis_size(axis)
        ends = count - 1
        head = lax.slice_in_dim(cells, 0, width, axis=dim)
        tail = lax.slice_in_dim(cells, cells.shape[dim] - width, cells.shape[dim], axis=dim)
        cells = jnp.concatenate(
            [
                lax.ppermute(tail, axis, [(i, (i + 1) % count) for i in range(ends)]),
                cells,
                lax.ppermute(head, axis, [((i + 1) % count, i) for i in range(ends)]),
            ],
            axis=dim,
        )
    return cells


def image_labels(positions, image_ends, all_tokens):
    inside = (positions >= 0) & (positions < all_tokens)
    counted = jnp.sum((positions[:, None] >= image_ends[None, :]).astype(jnp.int32), axis=1)
    return jnp.where(inside, counted, -1)


def body(qkv, residual_in, out_weight, merge_weight, merge_gain, image_groups, dest_row):
    width_here = qkv.shape[1]
    tok_rows = qkv.shape[2]
    heads_here = width_here // HEAD_DIM
    full_width = out_weight.shape[0]
    reach_rows = tok_rows // 2
    block_rows = min(1024, tok_rows)
    block_count = tok_rows // block_rows
    window = block_rows + 2 * reach_rows
    row_count = lax.axis_size("row")
    row_id = lax.axis_index("row")
    col_id = lax.axis_index("col")
    all_tokens = tok_rows * row_count
    score_scale = 1.0 / math.sqrt(HEAD_DIM)
    image_ends = jnp.cumsum(image_groups) * 4
    extended = with_halo(qkv[1:], (("row", 2),), reach_rows)
    positions = (
        row_id * tok_rows - reach_rows + jnp.arange(tok_rows + 2 * reach_rows, dtype=jnp.int32)
    )
    labels = image_labels(positions, image_ends, all_tokens)

    def attend(block_id):
        first_row = block_id * block_rows
        queries = lax.dynamic_slice_in_dim(qkv[0], first_row, block_rows, 1).reshape(
            heads_here, HEAD_DIM, block_rows
        )
        key_block = lax.dynamic_slice_in_dim(extended[0], first_row, window, 1).reshape(
            heads_here, HEAD_DIM, window
        )
        value_block = lax.dynamic_slice_in_dim(extended[1], first_row, window, 1).reshape(
            heads_here, HEAD_DIM, window
        )
        query_labels = lax.dynamic_slice_in_dim(labels, first_row + reach_rows, block_rows, 0)
        key_labels = lax.dynamic_slice_in_dim(labels, first_row, window, 0)
        scores = (
            jnp.einsum("hdq,hdk->hqk", queries, key_block, preferred_element_type=jnp.float32)
            * score_scale
        )
        same_image = (query_labels[:, None] == key_labels[None, :])[None]
        scores = jnp.where(same_image, scores, -1e30)
        row_max = jnp.max(scores, axis=2, keepdims=True)
        exponent = jnp.exp(scores - row_max)
        totals = jnp.sum(exponent, axis=2)
        weights = exponent.astype(jnp.bfloat16)
        weighted = jnp.einsum(
            "hqk,hdk->hdq", weights, value_block, preferred_element_type=jnp.float32
        )
        weighted = weighted / totals[:, None, :]
        return weighted.astype(jnp.bfloat16).reshape(width_here, block_rows)

    attended = lax.map(attend, jnp.arange(block_count, dtype=jnp.int32))
    attended = jnp.transpose(attended, (1, 0, 2)).reshape(width_here, tok_rows)
    head_weight = lax.dynamic_slice_in_dim(out_weight, col_id * width_here, width_here, 0)
    partial_value = lax.dot_general(
        head_weight, attended, (((0,), (0,)), ((), ())), preferred_element_type=jnp.float32
    )
    projected = lax.psum_scatter(partial_value, "col", scatter_dimension=0, tiled=True)
    layer_out = (residual_in.astype(jnp.float32) + projected).astype(jnp.bfloat16)
    full_rows = lax.all_gather(layer_out, "col", axis=0, tiled=True)
    values32 = full_rows.astype(jnp.float32)
    centre = jnp.mean(values32, axis=0, keepdims=True)
    spread = jnp.mean(jnp.square(values32 - centre), axis=0, keepdims=True)
    normed = ((values32 - centre) * lax.rsqrt(spread + 1e-06) * merge_gain[:, None]).astype(
        jnp.bfloat16
    )
    group_rows = tok_rows // 4
    grouped = normed.reshape(full_width, group_rows, 4)
    weight_parts = merge_weight.reshape(width_here, 4, full_width)
    merged = jnp.einsum(
        "ojf,fgj->og", weight_parts, grouped, preferred_element_type=jnp.float32
    ).astype(jnp.bfloat16)
    empty_rows = jnp.zeros((width_here, group_rows), jnp.bfloat16)
    every_row, every_dest = (
        lax.all_gather(merged, "row", axis=1, tiled=True),
        lax.all_gather(dest_row, "row", axis=0, tiled=True),
    )
    slot_index = every_dest - row_id * group_rows
    slot_index = jnp.where((slot_index >= 0) & (slot_index < group_rows), slot_index, group_rows)
    image_rows = empty_rows.at[:, slot_index].set(every_row, mode="drop")
    return (layer_out, image_rows)


def solution(mesh):
    return jax.shard_map(
        body,
        mesh=mesh,
        in_specs=(P(None, "col", "row"), P("col", "row"), P(), P("col", None), P(), P(), P("row")),
        out_specs=(P("col", "row"), P("col", "row")),
        check_vma=False,
    )
```

profile of v0, /device:TPU:0, one launch (start us, length us, event | category | flops | bytes accessed | tf_op | source)
XLA Modules:
  0.0 381.6 jit_solution(7010875313808431647)
XLA Ops:
  7.2 0.0 slice-start
  7.2 0.0 copy-start.5
  7.2 0.0 reduce-scatter.2.cloned.1.call-start
  7.2 2.4 fusion.44
  9.7 3.9 %collective-permute-start = (bf16[2,176,1024]{2,1,0:T(8,128)(2,1)}, bf16[2,176,1024]{2,1,0:T(8,128)(2,1)S(1)}, u32[]{:S(2)}, u32[]{:S(2)}) collective-permute-start(bf16[2,176,1024]{2,1,0:T(8,128)(2,1)} %get-tuple-element.106), channel_id=1, source_target_pairs={{0,8},{8,16},{16,24},{24,32},{32,40},{40,48},{48,56},{56,64},{64,7... | collective-permute-start | bytes 2162696 | tf_op jit(solution)/shard_map/ppermute | solution.py:18
  13.6 1.3 collective-permute-start.1
  14.9 0.0 copy-done.5
  15.0 0.1 copy.28
  15.1 0.1 reduce-window.8
  15.2 0.1 multiply_reduce_fusion
  15.3 0.2 convert_reduce_fusion.1
  15.5 13.8 %collective-permute-done = bf16[2,176,1024]{2,1,0:T(8,128)(2,1)S(1)} collective-permute-done((bf16[2,176,1024]{2,1,0:T(8,128)(2,1)}, bf16[2,176,1024]{2,1,0:T(8,128)(2,1)S(1)}, u32[]{:S(2)}, u32[]{:S(2)}) %collective-permute-start) | collective-permute-done | bytes 720928 | tf_op jit(solution)/shard_map/ppermute | solution.py:18
  29.3 4.1 %collective-permute-done.1 = bf16[2,176,1024]{2,1,0:T(8,128)(2,1)} collective-permute-done((bf16[2,176,1024]{2,1,0:T(8,128)(2,1)S(1)}, bf16[2,176,1024]{2,1,0:T(8,128)(2,1)}, u32[]{:S(2)}, u32[]{:S(2)}) %collective-permute-start.1) | collective-permute-done | bytes 720928 | tf_op jit(solution)/shard_map/ppermute | solution.py:20
  33.4 0.0 slice-done
  33.4 3.1 pad_maximum_fusion
  36.4 91.2 %while.12 = (s32[]{:T(128)}, bf16[2,176,1024]{2,1,0:T(8,128)(2,1)}, bf16[2,176,4096]{2,1,0:T(8,128)(2,1)}, s32[2]{0:T(128)S(1)}, s32[4096]{0:T(1024)S(1)}, /*ind...) while((s32[]{:T(128)}, bf16[2,176,1024]{2,1,0:T(8,128)(2,1)}, ...), condition=%wide.region_5.6_spmd, body=%wide.region_2.5_spmd.sunk | while | flops 2287300608 | bytes 108356392 | solution.py:83
  36.4 0.7 dynamic_slice.44
  37.8 2.0 broadcast_compare_fusion.2
  39.8 2.1 fusion.61
  41.9 1.6 constant_dynamic-slice_fusion.5
  43.6 1.2 slice.41
  44.8 12.6 %fusion.62 = (f32[2,1024]{1,0:T(2,128)S(1)}, f32[2,1024,3072]{2,1,0:T(8,128)}) fusion(pred[1024,3072]{1,0:T(8,128)(4,1)S(1)} %broadcast_compare_fusion.2, bf16[2,88,1024]{2,1,0:T(8,128)(2,1)S(1)} %bitcast.59, bf16[2,88,3072]{2,1,0:T(8,128)(2,1)} %bitcast.57), kind=kOutput, calls=%fused_computation.3.clone.1 | convolution fusion | flops 1126168576 | bytes 29761536 | tf_op jit(solution)/shard_map/while/body/eval_jaxpr/hdq,hdk->hqk/dot_general | solution.py:68
  57.4 0.0 copy-start.1
  57.4 12.0 %fusion.63 = f32[2,1024]{1,0:T(2,128)S(1)} fusion(f32[2,1024,3072]{2,1,0:T(8,128)} %get-tuple-element.155, f32[2,1024]{1,0:T(2,128)S(1)} %get-tuple-element.156, pred[1024,3072]{1,0:T(8,128)(4,1)S(1)} %broadcast_compare_fusion.2), kind=kLoop, calls=%fused_computation.4.clone.1 | loop fusion | flops 25163776 | bytes 28327936 | tf_op jit(solution)/shard_map/while/body/eval_jaxpr/reduce_sum | solution.py:75
  69.4 0.0 copy-done.1
  69.4 11.8 %fusion.64 = bf16[2,88,1024]{2,1,0:T(8,128)(2,1)S(1)} fusion(bf16[2,88,3072]{2,1,0:T(8,128)(2,1)S(1)} %bitcast.56, f32[2,1024,3072]{2,1,0:T(8,128)} %get-tuple-element.155, f32[2,1024]{1,0:T(2,128)S(1)} %get-tuple-element.156, pred[1024,3072]{1,0:T(8,128)(4,1)S(1)} %broadcast_compare_fusion.2, f32[2,1024]{1,0:T(2,128)S(1)} %fusion.63), kind=kOutput, calls=%fused_computation.10.clone.1 | convolution fusion | flops 1132822528 | bytes 29769728 | tf_op jit(solution)/shard_map/while/body/eval_jaxpr/hqk,hdk->hdq/dot_general | solution.py:77
  81.3 0.8 bitcast_dynamic-update-slice_fusion.2
  82.0 0.7 dynamic_slice.44
  83.4 2.0 broadcast_compare_fusion.2
  85.4 2.1 fusion.61
  87.5 1.6 constant_dynamic-slice_fusion.5
  89.2 1.2 slice.41
  90.4 12.6 %fusion.62 = (f32[2,1024]{1,0:T(2,128)S(1)}, f32[2,1024,3072]{2,1,0:T(8,128)}) fusion(pred[1024,3072]{1,0:T(8,128)(4,1)S(1)} %broadcast_compare_fusion.2, bf16[2,88,1024]{2,1,0:T(8,128)(2,1)S(1)} %bitcast.59, bf16[2,88,3072]{2,1,0:T(8,128)(2,1)} %bitcast.57), kind=kOutput, calls=%fused_computation.3.clone.1 | convolution fusion | flops 1126168576 | bytes 29761536 | tf_op jit(solution)/shard_map/while/body/eval_jaxpr/hdq,hdk->hqk/dot_general | solution.py:68
  103.0 12.0 %fusion.63 = f32[2,1024]{1,0:T(2,128)S(1)} fusion(f32[2,1024,3072]{2,1,0:T(8,128)} %get-tuple-element.155, f32[2,1024]{1,0:T(2,128)S(1)} %get-tuple-element.156, pred[1024,3072]{1,0:T(8,128)(4,1)S(1)} %broadcast_compare_fusion.2), kind=kLoop, calls=%fused_computation.4.clone.1 | loop fusion | flops 25163776 | bytes 28327936 | tf_op jit(solution)/shard_map/while/body/eval_jaxpr/reduce_sum | solution.py:75
  115.0 0.0 copy-done.1
  115.0 11.8 %fusion.64 = bf16[2,88,1024]{2,1,0:T(8,128)(2,1)S(1)} fusion(bf16[2,88,3072]{2,1,0:T(8,128)(2,1)S(1)} %bitcast.56, f32[2,1024,3072]{2,1,0:T(8,128)} %get-tuple-element.155, f32[2,1024]{1,0:T(2,128)S(1)} %get-tuple-element.156, pred[1024,3072]{1,0:T(8,128)(4,1)S(1)} %broadcast_compare_fusion.2, f32[2,1024]{1,0:T(2,128)S(1)} %fusion.63), kind=kOutput, calls=%fused_computation.10.clone.1 | convolution fusion | flops 1132822528 | bytes 29769728 | tf_op jit(solution)/shard_map/while/body/eval_jaxpr/hqk,hdk->hdq/dot_general | solution.py:77
  126.9 0.8 bitcast_dynamic-update-slice_fusion.2
  127.7 1.2 copy.36
  128.8 7.1 %fusion.38 = f32[1408,2048]{1,0:T(8,128)} fusion(bf16[176,2048]{1,0:T(8,128)(2,1)S(1)} %bitcast.61, bf16[1408,1408]{1,0:T(8,128)(2,1)} %param.11, s32[]{:T(128)S(6)} %select_n.41), kind=kOutput, calls=%fused_computation.34 | convolution fusion | flops 1015021568 | bytes 12750852 | tf_op jit(solution)/shard_map/dot_general | solution.py:86
  135.9 0.0 reduce-scatter.2.cloned.1.call-update
  135.9 0.2 all-gather.4.cloned.1.call-start
  136.2 70.0 %reduce-scatter.2.cloned.1.call-done = f32[176,2048]{1,0:T(8,128)} async-done(((f32[1408,2048]{1,0:T(8,128)}), f32[176,2048]{1,0:T(8,128)}) %reduce-scatter.2.cloned.1.call-update) | async-done | bytes 1441808 | tf_op jit(solution)/shard_map/reduce_scatter | solution.py:89
  206.2 0.0 copy-done.2
  206.2 2.4 add_convert_fusion
  208.6 0.0 all-gather.4.cloned.1.call-update
  208.6 0.0 copy-start.3
  208.6 0.0 all-gather.6.cloned.1.call-start
  208.7 38.4 %all-gather.4.cloned.1.call-done = bf16[1408,2048]{1,0:T(8,128)(2,1)} async-done(((bf16[176,2048]{1,0:T(8,128)(2,1)}), bf16[1408,2048]{1,0:T(8,128)(2,1)}) %all-gather.4.cloned.1.call-update) | async-done | bytes 5767184 | tf_op jit(solution)/shard_map/all_gather | solution.py:91
  247.1 3.7 convert_reduce_fusion
  250.8 0.6 copy-done
  251.4 1.5 fusion.16
  252.9 0.0 copy-done.3
  253.0 4.3 %fusion.18 = bf16[1408,2048]{1,0:T(8,128)(2,1)} fusion(bf16[1408,2048]{1,0:T(8,128)(2,1)S(1)} %copy-done, f32[1408]{0:T(1024)S(1)} %copy-done.3, f32[2048]{0:T(1024)S(1)} %add_rsqrt_fusion, f32[2048]{0:T(1024)S(1)} %broadcast_multiply_fusion), kind=kLoop, calls=%fused_computation.23 | loop fusion | flops 14417920 | bytes 11556352 | tf_op jit(solution)/shard_map/convert_element_type | solution.py:95
  257.2 8.4 %copy.30 = bf16[1408,2048]{0,1:T(8,128)(2,1)} copy(bf16[1408,2048]{1,0:T(8,128)(2,1)} %fusion.18) | data formatting | bytes 11534336 | tf_op jit(solution)/shard_map/convert_element_type | solution.py:95
  265.6 10.6 %reshape.116 = bf16[1408,512,4]{0,2,1:T(4,128)(2,1)} reshape(bf16[1408,2048]{0,1:T(8,128)(2,1)} %copy.30) | data formatting | bytes 11534336 | tf_op jit(solution)/shard_map/reshape | solution.py:99
  276.2 0.0 copy-done.6
  276.2 5.4 %fusion.33 = bf16[176,512]{1,0:T(8,128)(2,1)} fusion(bf16[1408,512,4]{0,2,1:T(4,128)(2,1)} %reshape.116, bf16[22,4,8,1408]{3,2,1,0:T(8,128)(2,1)S(1)} %bitcast.67), kind=kOutput, calls=%fused_computation.32 | convolution fusion | flops 1015111680 | bytes 7929856 | tf_op jit(solution)/shard_map/ojf,fgj->og/dot_general | solution.py:101
  281.6 0.0 all-gather.6.cloned.1.call-update
  281.7 0.0 copy-done.4
  281.7 23.5 %all-gather = s32[16,1,512]{2,1,0:T(1,128)S(1)} all-gather(s32[1,1,512]{2,1,0:T(1,128)S(1)} %bitcast.65), channel_id=1, replica_groups=mesh['row'=16,'col'=8] {'row'}, dimensions={0}, use_global_device_ids=true | all-gather | bytes 34816 | tf_op jit(solution)/shard_map/all_gather | solution.py:107
  305.2 28.1 %all-gather.6.cloned.1.call-done = bf16[176,8192]{1,0:T(8,128)(2,1)} async-done(((bf16[176,512]{1,0:T(8,128)(2,1)}), bf16[176,8192]{1,0:T(8,128)(2,1)}) %all-gather.6.cloned.1.call-update) | async-done | bytes 2883600 | tf_op jit(solution)/shard_map/all_gather | solution.py:106
  333.3 5.8 %copy.33 = bf16[8192,176]{1,0:T(8,128)(2,1)} copy(bf16[8192,176]{0,1:T(8,128)(2,1)} %bitcast.60) | data formatting | bytes 5767168 | tf_op jit(solution)/shard_map/all_gather | solution.py:106
  339.1 35.2 %scatter_custom_fusion = bf16[176,512]{0,1:T(8,128)(2,1)S(1)} fusion(s32[8192]{0:T(1024)S(1)} %compare_select_fusion, bf16[8192,176]{1,0:T(8,128)(2,1)} %copy.33, bf16[]{:T(256)} %constant.97.clone.1), kind=kCustom, calls=%fused_computation.36 | custom fusion | bytes 180736 | tf_op jit(solution)/shard_map/scatter | solution.py:111
  374.3 0.8 copy.34
  (19 shorter events, 0.2 us)
Async XLA Ops:
  7.2 26.2 %slice-start = ((bf16[3,176,2048]{2,1,0:T(8,128)(2,1)}), bf16[2,176,2048]{2,1,0:T(8,128)(2,1)S(1)}, s32[]{:S(2)}) async-start(bf16[3,176,2048]{2,1,0:T(8,128)(2,1)} %param.9), calls=%async_computation.4 | async-start | bytes 2883584 | tf_op jit(solution)/shard_map/slice | solution.py:48
  7.2 7.8 %copy-start.5 = (s32[64]{0:T(128)S(1)}, s32[64]{0:T(128)}, u32[]{:S(2)}) copy-start(s32[64]{0:T(128)} %param.14) | copy-start | bytes 772
  7.2 199.0 %reduce-scatter.2.cloned.1.call-start = ((), (), s32[]{:S(2)}) async-start(), calls=%async_computation.1 | async-start | bytes 12976128 | tf_op jit(solution)/shard_map/reduce_scatter | solution.py:89
  9.7 19.6 %collective-permute-start = (bf16[2,176,1024]{2,1,0:T(8,128)(2,1)}, bf16[2,176,1024]{2,1,0:T(8,128)(2,1)S(1)}, u32[]{:S(2)}, u32[]{:S(2)}) collective-permute-start(bf16[2,176,1024]{2,1,0:T(8,128)(2,1)} %get-tuple-element.106), channel_id=1, source_target_pairs={{0,8},{8,16},{16,24},{24,32},{32,40},{40,48},{48,56},{56,64},{64,7... | collective-permute-start | bytes 2162696 | tf_op jit(solution)/shard_map/ppermute | solution.py:18
  13.6 19.7 %collective-permute-start.1 = (bf16[2,176,1024]{2,1,0:T(8,128)(2,1)S(1)}, bf16[2,176,1024]{2,1,0:T(8,128)(2,1)}, u32[]{:S(2)}, u32[]{:S(2)}) collective-permute-start(bf16[2,176,1024]{2,1,0:T(8,128)(2,1)S(1)} %get-tuple-element.107), channel_id=1, source_target_pairs={{8,0},{16,8},{24,16},{32,24},{40,32},{48,40},{56,48},{64,56},{72,6... | collective-permute-start | bytes 2162696 | tf_op jit(solution)/shard_map/ppermute | solution.py:20
  57.4 12.0 %copy-start.1 = (bf16[1,176,3072]{2,1,0:T(8,128)(2,1)S(1)}, bf16[1,176,3072]{2,1,0:T(8,128)(2,1)}, u32[]{:S(2)}) copy-start(bf16[1,176,3072]{2,1,0:T(8,128)(2,1)} %get-tuple-element.153) | copy-start | bytes 3244036 | tf_op jit(solution)/shard_map/while
  103.0 12.0 %copy-start.1 = (bf16[1,176,3072]{2,1,0:T(8,128)(2,1)S(1)}, bf16[1,176,3072]{2,1,0:T(8,128)(2,1)}, u32[]{:S(2)}) copy-start(bf16[1,176,3072]{2,1,0:T(8,128)(2,1)} %get-tuple-element.153) | copy-start | bytes 3244036 | tf_op jit(solution)/shard_map/while
  135.9 70.3 %copy-start.2 = (bf16[176,2048]{1,0:T(8,128)(2,1)S(1)}, bf16[176,2048]{1,0:T(8,128)(2,1)}, u32[]{:S(2)}) copy-start(bf16[176,2048]{1,0:T(8,128)(2,1)} %param.10) | copy-start | bytes 2162692
  135.9 111.1 %all-gather.4.cloned.1.call-start = ((), (), s32[]{:S(2)}) async-start(), calls=%async_computation.2 | async-start | bytes 6488064 | tf_op jit(solution)/shard_map/all_gather | solution.py:91
  208.6 44.3 %copy-start.3 = (f32[1408]{0:T(1024)S(1)}, f32[1408]{0:T(1024)}, u32[]{:S(2)}) copy-start(f32[1408]{0:T(1024)} %param.13) | copy-start | bytes 16900
  208.6 124.7 %all-gather.6.cloned.1.call-start = ((), (), s32[]{:S(2)}) async-start(), calls=%async_computation.3 | async-start | bytes 3063808 | tf_op jit(solution)/shard_map/all_gather | solution.py:106
  247.1 4.3 %copy-start = (bf16[1408,2048]{1,0:T(8,128)(2,1)S(1)}, bf16[1408,2048]{1,0:T(8,128)(2,1)}, u32[]{:S(2)}) copy-start(bf16[1408,2048]{1,0:T(8,128)(2,1)} %all-gather.4.cloned.1.call-done) | copy-start | bytes 17301508
  265.6 10.7 %copy-start.6 = (bf16[176,5632]{1,0:T(8,128)(2,1)S(1)}, bf16[176,5632]{1,0:T(8,128)(2,1)}, u32[]{:S(2)}) copy-start(bf16[176,5632]{1,0:T(8,128)(2,1)} %param.12) | copy-start | bytes 5947396
  276.2 5.4 %copy-start.4 = (s32[512]{0:T(512)S(1)}, s32[512]{0:T(512)}, u32[]{:S(2)}) copy-start(s32[512]{0:T(512)} %param.15) | copy-start | bytes 6148
Sparse Core Ops, SparseCore 0:
  136.1 70.0 reduce-scatter.1
  208.7 38.2 all-gather.3
  281.8 51.4 all-gather.5
where the time goes:
time: 383 us; the launch traced here: 382 us
  waiting for transfers between devices  154 us (40%)
  local copies, waits for them, and re-layouts  77.9 us (20%)
  matrix products  61.4 us (16%)
  other arithmetic  43.4 us (11%)
  blocking collectives  23.5 us (6%)
  between operations  13.9 us (4%)
  starting transfers between devices  5.53 us (1%)
    reduce_scatter x1, waiting for transfers between devices, body(): lax.psum_scatter(partial_value, 'col', scatter_dimension=0, tiled=True)  70 us
    all_gather x1, waiting for transfers between devices, body(): full_rows = lax.all_gather(layer_out, 'col', axis=0, tiled=True)  38.4 us
    scatter x1, local copies, waits for them, and re-layouts, body(): image_rows = empty_rows.at[:, slot_index].set(every_row, mode='drop')  35.2 us
    all_gather x1, waiting for transfers between devices, body(): lax.all_gather(merged, 'row', axis=1, tiled=True)  28.1 us
    dot_general x2, matrix products, attend(): jnp.einsum('hdq,hdk->hqk', queries, key_block, preferred_element_type=jnp...  25.3 us
    reduce_sum x2, other arithmetic, attend(): totals = jnp.sum(exponent, axis=2)  24 us
    dot_general x2, matrix products, attend(): jnp.einsum('hqk,hdk->hdq', weights, value_block, preferred_element_type=j...  23.7 us
    all_gather x1, blocking collectives, body(): lax.all_gather(dest_row, 'row', axis=0, tiled=True)  23.5 us
  transfers between devices with their start and end apart: 5, of which 5 were waited for; matrix products, arithmetic and copies ran while one was open for 0% of the time, Pallas kernels for 0%

commit v1 on v0

--- a/solution.py
+++ b/solution.py
@@ -103,7 +103,9 @@
     ).astype(jnp.bfloat16)
     empty_rows = jnp.zeros((width_here, group_rows), jnp.bfloat16)
     every_row, every_dest = (
-        lax.all_gather(merged, "row", axis=1, tiled=True),
+        jnp.concatenate(
+            lax.all_to_all(jnp.stack([merged] * lax.axis_size("row")), "row", 0, 0), axis=1
+        ),
         lax.all_gather(dest_row, "row", axis=0, tiled=True),
     )
     slot_index = every_dest - row_id * group_rows

time: 383 us -> 399 us (1.042)
  blocking collectives: 23.5 us -> 56.2 us
  waiting for transfers between devices: 154 us -> 126 us
  starting transfers between devices: 5.53 us -> 12.4 us
    all_gather x1, blocking collectives: 23.5 us -> 56.2 us  [body(): lax.all_gather(dest_row, 'row', axis=0, tiled=True)]
    all_gather x1 -> x0, waiting for transfers between devices: 28.1 us -> none  [body(): lax.all_gather(merged, 'row', axis=1, tiled=True)]
    all_to_all x0 -> x1, starting transfers between devices: none -> 6.94 us  [body(): lax.all_to_all(jnp.stack([merged] * lax.axis_size('row')), 'row', 0, 0)]
    reshape x0 -> x2, local copies, waits for them, and re-layouts: none -> 6.02 us  [body(): jnp.concatenate(lax.all_to_all(jnp.stack([merged] * lax.axis_size('row'))...]
    all_gather x1 -> x0, local copies, waits for them, and re-layouts: 5.8 us -> none  [body(): lax.all_gather(merged, 'row', axis=1, tiled=True)]
  transfers between devices with their start and end apart: 5 -> 5, of which waited for: 5 -> 4; matrix products, arithmetic and copies ran while one was open for 0% -> 0% of each run, Pallas kernels for 0% -> 0%
where the time goes in v1:
time: 399 us; the launch traced here: 396 us
  waiting for transfers between devices  126 us (32%)
  local copies, waits for them, and re-layouts  81.5 us (20%)
  matrix products  60.8 us (15%)
  blocking collectives  56.2 us (14%)
  other arithmetic  43.4 us (11%)
  between operations  14.2 us (4%)
  starting transfers between devices  12.4 us (3%)
    reduce_scatter x1, waiting for transfers between devices, body(): lax.psum_scatter(partial_value, 'col', scatter_dimension=0, tiled=True)  70 us
    all_gather x1, blocking collectives, body(): lax.all_gather(dest_row, 'row', axis=0, tiled=True)  56.2 us
    all_gather x1, waiting for transfers between devices, body(): full_rows = lax.all_gather(layer_out, 'col', axis=0, tiled=True)  38.4 us
    scatter x1, local copies, waits for them, and re-layouts, body(): image_rows = empty_rows.at[:, slot_index].set(every_row, mode='drop')  35.2 us
    dot_general x2, matrix products, attend(): jnp.einsum('hdq,hdk->hqk', queries, key_block, preferred_element_type=jnp...  25.3 us
    reduce_sum x2, other arithmetic, attend(): totals = jnp.sum(exponent, axis=2)  24 us
    dot_general x2, matrix products, attend(): jnp.einsum('hqk,hdk->hdq', weights, value_block, preferred_element_type=j...  23.7 us
    ppermute x1, waiting for transfers between devices, with_halo(): lax.ppermute(tail, axis, [(i, (i + 1) % count) for i in range(ends)])  13.8 us
  transfers between devices with their start and end apart: 5, of which 4 were waited for; matrix products, arithmetic and copies ran while one was open for 0% of the time, Pallas kernels for 0%

profile of v1, /device:TPU:0, one launch (start us, length us, event | category | flops | bytes accessed | tf_op | source)
XLA Modules:
  0.0 396.4 jit_solution(1716384186507280638)
XLA Ops:
  7.2 0.0 slice-start
  7.2 0.0 copy-start.6
  7.2 0.0 reduce-scatter.2.cloned.1.call-start
  7.2 2.4 fusion.44
  9.7 3.9 collective-permute-start
  13.6 1.3 collective-permute-start.1
  14.9 0.0 copy-done.6
  15.0 0.1 copy.35
  15.1 0.1 reduce-window.8
  15.2 0.1 multiply_reduce_fusion
  15.3 0.2 convert_reduce_fusion.1
  15.5 13.8 %collective-permute-done = bf16[2,176,1024]{2,1,0:T(8,128)(2,1)S(1)} collective-permute-done((bf16[2,176,1024]{2,1,0:T(8,128)(2,1)}, bf16[2,176,1024]{2,1,0:T(8,128)(2,1)S(1)}, u32[]{:S(2)}, u32[]{:S(2)}) %collective-permute-start) | collective-permute-done | bytes 720928 | tf_op jit(solution)/shard_map/ppermute | solution.py:18
  29.3 4.1 %collective-permute-done.1 = bf16[2,176,1024]{2,1,0:T(8,128)(2,1)} collective-permute-done((bf16[2,176,1024]{2,1,0:T(8,128)(2,1)S(1)}, bf16[2,176,1024]{2,1,0:T(8,128)(2,1)}, u32[]{:S(2)}, u32[]{:S(2)}) %collective-permute-start.1) | collective-permute-done | bytes 720928 | tf_op jit(solution)/shard_map/ppermute | solution.py:20
  33.4 0.0 slice-done
  33.4 3.1 pad_maximum_fusion
  36.4 91.2 %while.12 = (s32[]{:T(128)}, bf16[2,176,1024]{2,1,0:T(8,128)(2,1)}, bf16[2,176,4096]{2,1,0:T(8,128)(2,1)}, s32[2]{0:T(128)S(1)}, s32[4096]{0:T(1024)S(1)}, /*ind...) while((s32[]{:T(128)}, bf16[2,176,1024]{2,1,0:T(8,128)(2,1)}, ...), condition=%wide.region_5.6_spmd, body=%wide.region_2.5_spmd.sunk | while | flops 2287300608 | bytes 108356392 | solution.py:83
  36.4 0.7 dynamic_slice.44
  37.8 2.0 broadcast_compare_fusion.2
  39.8 2.1 fusion.61
  41.9 1.6 constant_dynamic-slice_fusion.5
  43.6 1.2 slice.41
  44.8 12.6 %fusion.62 = (f32[2,1024]{1,0:T(2,128)S(1)}, f32[2,1024,3072]{2,1,0:T(8,128)}) fusion(pred[1024,3072]{1,0:T(8,128)(4,1)S(1)} %broadcast_compare_fusion.2, bf16[2,88,1024]{2,1,0:T(8,128)(2,1)S(1)} %bitcast.65, bf16[2,88,3072]{2,1,0:T(8,128)(2,1)} %bitcast.61), kind=kOutput, calls=%fused_computation.3.clone.1 | convolution fusion | flops 1126168576 | bytes 29761536 | tf_op jit(solution)/shard_map/while/body/eval_jaxpr/hdq,hdk->hqk/dot_general | solution.py:68
  57.4 12.0 %fusion.63 = f32[2,1024]{1,0:T(2,128)S(1)} fusion(f32[2,1024,3072]{2,1,0:T(8,128)} %get-tuple-element.157, f32[2,1024]{1,0:T(2,128)S(1)} %get-tuple-element.158, pred[1024,3072]{1,0:T(8,128)(4,1)S(1)} %broadcast_compare_fusion.2), kind=kLoop, calls=%fused_computation.4.clone.1 | loop fusion | flops 25163776 | bytes 28327936 | tf_op jit(solution)/shard_map/while/body/eval_jaxpr/reduce_sum | solution.py:75
  69.4 0.0 copy-done.1
  69.4 11.8 %fusion.64 = bf16[2,88,1024]{2,1,0:T(8,128)(2,1)S(1)} fusion(bf16[2,88,3072]{2,1,0:T(8,128)(2,1)S(1)} %bitcast.60, f32[2,1024,3072]{2,1,0:T(8,128)} %get-tuple-element.157, f32[2,1024]{1,0:T(2,128)S(1)} %get-tuple-element.158, pred[1024,3072]{1,0:T(8,128)(4,1)S(1)} %broadcast_compare_fusion.2, f32[2,1024]{1,0:T(2,128)S(1)} %fusion.63), kind=kOutput, calls=%fused_computation.10.clone.1 | convolution fusion | flops 1132822528 | bytes 29769728 | tf_op jit(solution)/shard_map/while/body/eval_jaxpr/hqk,hdk->hdq/dot_general | solution.py:77
  81.3 0.8 bitcast_dynamic-update-slice_fusion.2
  82.0 0.7 dynamic_slice.44
  83.4 2.0 broadcast_compare_fusion.2
  85.4 2.1 fusion.61
  87.5 1.6 constant_dynamic-slice_fusion.5
  89.2 1.2 slice.41
  90.4 12.6 %fusion.62 = (f32[2,1024]{1,0:T(2,128)S(1)}, f32[2,1024,3072]{2,1,0:T(8,128)}) fusion(pred[1024,3072]{1,0:T(8,128)(4,1)S(1)} %broadcast_compare_fusion.2, bf16[2,88,1024]{2,1,0:T(8,128)(2,1)S(1)} %bitcast.65, bf16[2,88,3072]{2,1,0:T(8,128)(2,1)} %bitcast.61), kind=kOutput, calls=%fused_computation.3.clone.1 | convolution fusion | flops 1126168576 | bytes 29761536 | tf_op jit(solution)/shard_map/while/body/eval_jaxpr/hdq,hdk->hqk/dot_general | solution.py:68
  103.0 12.0 %fusion.63 = f32[2,1024]{1,0:T(2,128)S(1)} fusion(f32[2,1024,3072]{2,1,0:T(8,128)} %get-tuple-element.157, f32[2,1024]{1,0:T(2,128)S(1)} %get-tuple-element.158, pred[1024,3072]{1,0:T(8,128)(4,1)S(1)} %broadcast_compare_fusion.2), kind=kLoop, calls=%fused_computation.4.clone.1 | loop fusion | flops 25163776 | bytes 28327936 | tf_op jit(solution)/shard_map/while/body/eval_jaxpr/reduce_sum | solution.py:75
  115.0 0.0 copy-done.1
  115.0 11.8 %fusion.64 = bf16[2,88,1024]{2,1,0:T(8,128)(2,1)S(1)} fusion(bf16[2,88,3072]{2,1,0:T(8,128)(2,1)S(1)} %bitcast.60, f32[2,1024,3072]{2,1,0:T(8,128)} %get-tuple-element.157, f32[2,1024]{1,0:T(2,128)S(1)} %get-tuple-element.158, pred[1024,3072]{1,0:T(8,128)(4,1)S(1)} %broadcast_compare_fusion.2, f32[2,1024]{1,0:T(2,128)S(1)} %fusion.63), kind=kOutput, calls=%fused_computation.10.clone.1 | convolution fusion | flops 1132822528 | bytes 29769728 | tf_op jit(solution)/shard_map/while/body/eval_jaxpr/hqk,hdk->hdq/dot_general | solution.py:77
  126.9 0.8 bitcast_dynamic-update-slice_fusion.2
  127.7 1.2 copy.44
  128.8 7.1 %fusion.38 = f32[1408,2048]{1,0:T(8,128)} fusion(bf16[176,2048]{1,0:T(8,128)(2,1)S(1)} %bitcast.66, bf16[1408,1408]{1,0:T(8,128)(2,1)} %param.11, s32[]{:T(128)S(6)} %select_n.41), kind=kOutput, calls=%fused_computation.34 | convolution fusion | flops 1015021568 | bytes 12750852 | tf_op jit(solution)/shard_map/dot_general | solution.py:86
  135.9 0.0 reduce-scatter.2.cloned.1.call-update
  135.9 0.2 all-gather.3.cloned.1.call-start
  136.2 70.0 %reduce-scatter.2.cloned.1.call-done = f32[176,2048]{1,0:T(8,128)} async-done(((f32[1408,2048]{1,0:T(8,128)}), f32[176,2048]{1,0:T(8,128)}) %reduce-scatter.2.cloned.1.call-update) | async-done | bytes 1441808 | tf_op jit(solution)/shard_map/reduce_scatter | solution.py:89
  206.2 0.0 copy-done.3
  206.2 2.4 add_convert_fusion
  208.6 0.0 all-gather.3.cloned.1.call-update
  208.6 0.0 copy-start.4
  208.6 38.4 %all-gather.3.cloned.1.call-done = bf16[1408,2048]{1,0:T(8,128)(2,1)} async-done(((bf16[176,2048]{1,0:T(8,128)(2,1)}), bf16[1408,2048]{1,0:T(8,128)(2,1)}) %all-gather.3.cloned.1.call-update) | async-done | bytes 5767184 | tf_op jit(solution)/shard_map/all_gather | solution.py:91
  247.1 3.7 convert_reduce_fusion
  250.8 0.6 copy-done
  251.4 1.5 fusion.16
  253.0 4.3 %fusion.18 = bf16[1408,2048]{1,0:T(8,128)(2,1)} fusion(bf16[1408,2048]{1,0:T(8,128)(2,1)S(1)} %copy-done, f32[1408]{0:T(1024)S(1)} %copy-done.4, f32[2048]{0:T(1024)S(1)} %add_rsqrt_fusion, f32[2048]{0:T(1024)S(1)} %broadcast_multiply_fusion), kind=kLoop, calls=%fused_computation.23 | loop fusion | flops 14417920 | bytes 11556352 | tf_op jit(solution)/shard_map/convert_element_type | solution.py:95
  257.2 8.4 %copy.37 = bf16[1408,2048]{0,1:T(8,128)(2,1)} copy(bf16[1408,2048]{1,0:T(8,128)(2,1)} %fusion.18) | data formatting | bytes 11534336 | tf_op jit(solution)/shard_map/convert_element_type | solution.py:95
  265.6 10.6 %reshape.124 = bf16[1408,512,4]{0,2,1:T(4,128)(2,1)} reshape(bf16[1408,2048]{0,1:T(8,128)(2,1)} %copy.37) | data formatting | bytes 11534336 | tf_op jit(solution)/shard_map/reshape | solution.py:99
  276.2 4.7 %fusion.33 = bf16[176,512]{1,0:T(8,128)(2,1)S(1)} fusion(bf16[1408,512,4]{0,2,1:T(4,128)(2,1)} %reshape.124, bf16[22,4,8,1408]{3,2,1,0:T(8,128)(2,1)S(1)} %bitcast.72), kind=kOutput, calls=%fused_computation.32 | convolution fusion | flops 1015111680 | bytes 7929856 | tf_op jit(solution)/shard_map/ojf,fgj->og/dot_general | solution.py:101
  281.0 0.0 copy-start.5
  281.0 1.9 stack.2
  282.8 6.9 %all-to-all-start = ((bf16[16,176,512]{2,1,0:T(8,128)(2,1)}), bf16[16,176,512]{2,1,0:T(8,128)(2,1)S(1)}, u32[]{:S(2)}, u32[]{:S(2)}) async-start(bf16[16,176,512]{2,1,0:T(8,128)(2,1)} %stack.2), calls=%async_computation.1 | async-start | bytes 5767168 | tf_op jit(solution)/shard_map/all_to_all | solution.py:107
  289.8 56.2 %all-gather = s32[16,1,512]{2,1,0:T(1,128)S(1)} all-gather(s32[1,1,512]{2,1,0:T(1,128)S(1)} %bitcast.70), channel_id=1, replica_groups=mesh['row'=16,'col'=8] {'row'}, dimensions={0}, use_global_device_ids=true | all-gather | bytes 34816 | tf_op jit(solution)/shard_map/all_gather | solution.py:109
  346.0 0.0 all-to-all-done
  346.0 0.0 copy-start.2
  346.0 1.6 copy-done.2
  347.6 2.1 copy.45
  349.8 3.9 copy.41
  353.6 35.2 %scatter_custom_fusion = bf16[176,512]{0,1:T(8,128)(2,1)S(1)} fusion(s32[8192]{0:T(1024)S(1)} %compare_select_fusion, bf16[8192,176]{1,0:T(8,128)(2,1)} %copy.41, bf16[]{:T(256)} %constant.97.clone.1), kind=kCustom, calls=%fused_computation.36 | custom fusion | bytes 180736 | tf_op jit(solution)/shard_map/scatter | solution.py:113
  388.8 0.8 copy.42
  (22 shorter events, 0.2 us)
Async XLA Ops:
  7.2 26.2 %slice-start = ((bf16[3,176,2048]{2,1,0:T(8,128)(2,1)}), bf16[2,176,2048]{2,1,0:T(8,128)(2,1)S(1)}, s32[]{:S(2)}) async-start(bf16[3,176,2048]{2,1,0:T(8,128)(2,1)} %param.9), calls=%async_computation.4 | async-start | bytes 2883584 | tf_op jit(solution)/shard_map/slice | solution.py:48
  7.2 7.8 %copy-start.6 = (s32[64]{0:T(128)S(1)}, s32[64]{0:T(128)}, u32[]{:S(2)}) copy-start(s32[64]{0:T(128)} %param.14) | copy-start | bytes 772
  7.2 199.0 %reduce-scatter.2.cloned.1.call-start = ((), (), s32[]{:S(2)}) async-start(), calls=%async_computation.2 | async-start | bytes 12976128 | tf_op jit(solution)/shard_map/reduce_scatter | solution.py:89
  9.7 19.6 %collective-permute-start = (bf16[2,176,1024]{2,1,0:T(8,128)(2,1)}, bf16[2,176,1024]{2,1,0:T(8,128)(2,1)S(1)}, u32[]{:S(2)}, u32[]{:S(2)}) collective-permute-start(bf16[2,176,1024]{2,1,0:T(8,128)(2,1)} %get-tuple-element.108), channel_id=1, source_target_pairs={{0,8},{8,16},{16,24},{24,32},{32,40},{40,48},{48,56},{56,64},{64,7... | collective-permute-start | bytes 2162696 | tf_op jit(solution)/shard_map/ppermute | solution.py:18
  13.6 19.7 %collective-permute-start.1 = (bf16[2,176,1024]{2,1,0:T(8,128)(2,1)S(1)}, bf16[2,176,1024]{2,1,0:T(8,128)(2,1)}, u32[]{:S(2)}, u32[]{:S(2)}) collective-permute-start(bf16[2,176,1024]{2,1,0:T(8,128)(2,1)S(1)} %get-tuple-element.109), channel_id=1, source_target_pairs={{8,0},{16,8},{24,16},{32,24},{40,32},{48,40},{56,48},{64,56},{72,6... | collective-permute-start | bytes 2162696 | tf_op jit(solution)/shard_map/ppermute | solution.py:20
  57.4 12.0 %copy-start.1 = (bf16[1,176,3072]{2,1,0:T(8,128)(2,1)S(1)}, bf16[1,176,3072]{2,1,0:T(8,128)(2,1)}, u32[]{:S(2)}) copy-start(bf16[1,176,3072]{2,1,0:T(8,128)(2,1)} %get-tuple-element.155) | copy-start | bytes 3244036 | tf_op jit(solution)/shard_map/while
  103.0 12.0 %copy-start.1 = (bf16[1,176,3072]{2,1,0:T(8,128)(2,1)S(1)}, bf16[1,176,3072]{2,1,0:T(8,128)(2,1)}, u32[]{:S(2)}) copy-start(bf16[1,176,3072]{2,1,0:T(8,128)(2,1)} %get-tuple-element.155) | copy-start | bytes 3244036 | tf_op jit(solution)/shard_map/while
  135.9 70.3 %copy-start.3 = (bf16[176,2048]{1,0:T(8,128)(2,1)S(1)}, bf16[176,2048]{1,0:T(8,128)(2,1)}, u32[]{:S(2)}) copy-start(bf16[176,2048]{1,0:T(8,128)(2,1)} %param.10) | copy-start | bytes 2162692
  135.9 111.1 %all-gather.3.cloned.1.call-start = ((), (), s32[]{:S(2)}) async-start(), calls=%async_computation.3 | async-start | bytes 6488064 | tf_op jit(solution)/shard_map/all_gather | solution.py:91
  208.6 44.3 %copy-start.4 = (f32[1408]{0:T(1024)S(1)}, f32[1408]{0:T(1024)}, u32[]{:S(2)}) copy-start(f32[1408]{0:T(1024)} %param.13) | copy-start | bytes 16900
  247.1 4.3 %copy-start = (bf16[1408,2048]{1,0:T(8,128)(2,1)S(1)}, bf16[1408,2048]{1,0:T(8,128)(2,1)}, u32[]{:S(2)}) copy-start(bf16[1408,2048]{1,0:T(8,128)(2,1)} %all-gather.3.cloned.1.call-done) | copy-start | bytes 17301508
  265.6 10.7 %copy-start.7 = (bf16[176,5632]{1,0:T(8,128)(2,1)S(1)}, bf16[176,5632]{1,0:T(8,128)(2,1)}, u32[]{:S(2)}) copy-start(bf16[176,5632]{1,0:T(8,128)(2,1)} %param.12) | copy-start | bytes 5947396
  281.0 8.8 %copy-start.5 = (s32[512]{0:T(512)S(1)}, s32[512]{0:T(512)}, u32[]{:S(2)}) copy-start(s32[512]{0:T(512)} %param.15) | copy-start | bytes 6148
  282.8 63.2 %all-to-all-start = ((bf16[16,176,512]{2,1,0:T(8,128)(2,1)}), bf16[16,176,512]{2,1,0:T(8,128)(2,1)S(1)}, u32[]{:S(2)}, u32[]{:S(2)}) async-start(bf16[16,176,512]{2,1,0:T(8,128)(2,1)} %stack.2), calls=%async_computation.1 | async-start | bytes 5767168 | tf_op jit(solution)/shard_map/all_to_all | solution.py:107
  346.0 1.6 copy-start.2
Sparse Core Ops, SparseCore 0:
  136.1 70.0 reduce-scatter.1
  208.7 38.2 all-gather.2
